TPU v7x, 32 devices: a whole 2x2x4 slice. The times are simulated.
32 devices in a mesh: groups: 2 (over x), ctx: 16 (over z, y, core).
Axes of the slice: x: 2, y: 2, z: 4, core: 2. Of those that a mesh axis runs over, the one named last changes fastest.
Arguments:
- q_latent: bfloat16 [128, 1536], P(('groups', 'ctx')), parts along dimension 0, may hold values from -64 to 64
- q_gain: float32 [1536], replicated, may hold values from 0.1 to 1.9
- w_uq: bfloat16 [1536, 24576], P(None, 'ctx'), may hold values from -0.15625 to 0.15625
- w_uk: bfloat16 [128, 128, 512], P('ctx'), may hold values from -0.5 to 0.5
- w_uv: bfloat16 [128, 512, 128], P('ctx'), may hold values from -0.25 to 0.25
- w_o: bfloat16 [16384, 7168], P('ctx'), may hold values from -0.046875 to 0.046875
- latent_cache: bfloat16 [65536, 576], P(('groups', 'ctx')), parts along dimension 0, may hold values from -1024 to 1024
- kv_scales: float32 [65536, 4], P(('groups', 'ctx')), parts along dimension 0, may hold values from 0.5 to 2
- selected: int32 [128, 32], P(('groups', 'ctx')), parts along dimension 0, may hold values from 0 to 511, as said below
- counts: int32 [128], P(('groups', 'ctx')), parts along dimension 0, may hold values from 8 to 32
Outputs:
- attn_out: bfloat16 [128, 7168], P(('groups', 'ctx')), parts along dimension 0
There are 2 independent parts, one for each index of `groups`. A program takes and returns all parts, laid end to end along the dimension named above; an argument that names none is the same for every part. Nothing has to cross between parts.
Inputs may be any that keep to these rules, and one draw needn't show every extreme that they name: `selected`: each row lists 32 different block numbers. Over the rows 4 i to 4 i + 4 - 1 (the query tokens of one device) and their first counts entries, at most 8 different listed blocks lie in the range 32 j to 32 j + 31 for any j.
All inputs are finite; a program needn't handle non-finite values.
Results may differ from a plain program's by a relative error of at most 0.01.
The roundings to bfloat16 on the way count: a program that leaves them out, or rounds other values in their place, can miss the bound.
Values may be sent and summed in bfloat16 or wider, within the bound.
A program may use at most 128 MiB of HBM per device.

v0:
```python
import math
import jax
import jax.numpy as jnp
from jax import lax
from jax.sharding import PartitionSpec as P

BLK = 64
norm_eps = 1e-06
rope_base = 10000.0


def rotate_rotary(rotary, positions):
    half_width = rotary.shape[-1] // 2
    freq_index = jnp.arange(half_width, dtype=jnp.float32)
    inverse_freq = jnp.exp(freq_index * (-2.0 * math.log(rope_base) / rotary.shape[-1]))
    angles = positions[:, None] * inverse_freq[None, :]
    cosine = jnp.cos(angles)[:, None, :]
    sine = jnp.sin(angles)[:, None, :]
    first_half = rotary[:, :, :half_width]
    second_half = rotary[:, :, half_width:]
    return jnp.concatenate(
        [first_half * cosine - second_half * sine, first_half * sine + second_half * cosine], axis=2
    )


def local(q_latent, q_gain, w_uq, w_uk, w_uv, w_o, latent_cache, kv_scales, selected, counts):
    n_devices = lax.axis_size("ctx")
    heads_local = w_uk.shape[0]
    width_content = w_uk.shape[1]
    width_latent = w_uk.shape[2]
    width_rotary = latent_cache.shape[1] - width_latent
    width_row = width_latent + width_rotary
    q_local = q_latent.shape[0]
    top_blocks = selected.shape[1]
    block_len = BLK
    blocks_local = latent_cache.shape[0] // block_len
    blocks_total = blocks_local * n_devices
    capacity = max(2, 4 * top_blocks // n_devices)
    latent_f = q_latent.astype(jnp.float32)
    normed = (
        latent_f
        * lax.rsqrt(jnp.mean(latent_f * latent_f, axis=1, keepdims=True) + norm_eps)
        * q_gain
    ).astype(jnp.bfloat16)
    scaled = (
        latent_cache[:, :width_latent].astype(jnp.float32)
        * jnp.repeat(kv_scales, width_latent // kv_scales.shape[1], axis=1)
    ).astype(jnp.bfloat16)
    cache_blocks = jnp.concatenate([scaled, latent_cache[:, width_latent:]], axis=1).reshape(
        blocks_local, block_len, width_row
    )
    live_sel = jnp.arange(top_blocks, dtype=jnp.int32)[None, :] < counts[:, None]
    block_match = selected[:, :, None] == jnp.arange(blocks_total, dtype=jnp.int32)[None, None, :]
    needed = (
        jnp.any(block_match & live_sel[:, :, None], axis=(0, 1))
        .reshape(n_devices, blocks_local)
        .astype(jnp.int32)
    )
    order_rank = jnp.cumsum(needed, axis=1) - 1
    slot_match = (needed[:, :, None] == 1) & (
        order_rank[:, :, None] == jnp.arange(capacity, dtype=jnp.int32)[None, None, :]
    )
    requests = jnp.sum(
        jnp.where(slot_match, jnp.arange(blocks_local, dtype=jnp.int32)[None, :, None], 0), axis=1
    )
    rank_flat = order_rank.reshape(blocks_total)
    sel_rank = jnp.sum(jnp.where(block_match, rank_flat[None, None, :], 0), axis=2)
    slot_index = jnp.where(live_sel, selected // blocks_local * capacity + sel_rank, 0)
    shard_piece = lax.all_gather(normed, "ctx", axis=0, tiled=True)
    row_count = shard_piece.shape[0]
    projected = jnp.dot(shard_piece, w_uq, preferred_element_type=jnp.float32).reshape(
        row_count, heads_local, width_content + width_rotary
    )
    content = projected[:, :, :width_content].astype(jnp.bfloat16)
    positions = jnp.arange(row_count, dtype=jnp.int32).astype(jnp.float32)
    rotated = rotate_rotary(projected[:, :, width_content:], positions).astype(jnp.bfloat16)
    absorbed = jnp.einsum("khn,hnc->khc", content, w_uk, preferred_element_type=jnp.float32).astype(
        jnp.bfloat16
    )
    head_queries = jnp.concatenate([absorbed, rotated], axis=2)
    queries = lax.all_to_all(head_queries, "ctx", split_axis=0, concat_axis=1, tiled=True)
    served = cache_blocks[lax.all_to_all(requests, "ctx", split_axis=0, concat_axis=0, tiled=True)]
    fetched = lax.all_to_all(served, "ctx", split_axis=0, concat_axis=0, tiled=True)
    fetched_rows = fetched.reshape(n_devices * capacity * block_len, width_row)
    token_index = (
        slot_index[:, :, None] * block_len + jnp.arange(block_len, dtype=jnp.int32)[None, None, :]
    ).reshape(q_local, top_blocks * block_len)
    live_tokens = jnp.repeat(live_sel, block_len, axis=1)
    softmax_scale = 1.0 / math.sqrt(width_content + width_rotary)

    def attend(inputs):
        query_row, token_rows, live_row = inputs
        key_rows = fetched_rows[token_rows]
        scores = jnp.dot(query_row, key_rows.T, preferred_element_type=jnp.float32) * softmax_scale
        scores = jnp.where(live_row[None, :], scores, -jnp.inf)
        row_peak = jnp.max(scores, axis=1, keepdims=True)
        exponent = jnp.exp(scores - row_peak)
        weights = (exponent / jnp.sum(exponent, axis=1, keepdims=True)).astype(jnp.bfloat16)
        return jnp.dot(
            weights, key_rows[:, :width_latent], preferred_element_type=jnp.float32
        ).astype(jnp.bfloat16)

    latent_out = lax.map(attend, (queries, token_index, live_tokens))
    head_out = lax.all_to_all(latent_out, "ctx", split_axis=1, concat_axis=0, tiled=True)
    head_values = jnp.einsum(
        "qhc,hcv->qhv", head_out, w_uv, preferred_element_type=jnp.float32
    ).astype(jnp.bfloat16)
    head_values = head_values.reshape(head_values.shape[0], heads_local * w_uv.shape[2])
    return lax.psum_scatter(
        jnp.dot(head_values, w_o, preferred_element_type=jnp.float32),
        "ctx",
        scatter_dimension=0,
        tiled=True,
    ).astype(jnp.bfloat16)


def solution(mesh):
    in_specs = (
        P(("groups", "ctx"), None),
        P(),
        P(None, "ctx"),
        P("ctx", None, None),
        P("ctx", None, None),
        P("ctx", None),
        P(("groups", "ctx"), None),
        P(("groups", "ctx"), None),
        P(("groups", "ctx"), None),
        P(("groups", "ctx")),
    )
    out_specs = P(("groups", "ctx"), None)
    return jax.shard_map(local, mesh=mesh, in_specs=in_specs, out_specs=out_specs, check_vma=False)
```

profile of v0, /device:TPU:0, one launch (start us, length us, event | category | flops | bytes accessed | tf_op | source)
XLA Modules:
  0.0 466.6 jit_solution(13454047989507777395)
XLA Ops:
  2.9 7.4 %all-to-all-start.1 = ((s32[16,1,8]{2,1,0:T(1,128)}), s32[16,1,8]{2,1,0:T(1,128)S(1)}, u32[]{:S(2)}, u32[]{:S(2)}) async-start(s32[16,1,8]{2,1,0:T(1,128)} %bitcast.18), calls=%async_computation.1 | async-start | bytes 16384 | tf_op jit(solution)/shard_map/all_to_all | solution.py:82
  12.0 22.2 %all-gather = bf16[16,4,1536]{2,1,0:T(4,128)(2,1)S(1)} all-gather(bf16[1,4,1536]{2,1,0:T(4,128)(2,1)S(1)} %fusion.30), channel_id=1, replica_groups=mesh['groups'=2,'ctx'=16] {'ctx'}, dimensions={0}, use_global_device_ids=true | all-gather | bytes 208896 | tf_op jit(solution)/shard_map/all_gather | solution.py:69
  34.2 3.3 fusion.39
  38.6 1.2 copy.45
  40.4 2.5 copy.59
  44.0 4.3 all-to-all-start
  48.2 4.7 %broadcast_in_dim.79 = f32[2048,4,128]{2,1,0:T(4,128)S(1)} broadcast(f32[2048,4]{1,0:T(8,128)S(1)} %copy.48), dimensions={0,1} | broadcast | bytes 4227072 | tf_op jit(solution)/shard_map/broadcast_in_dim | solution.py:47
  54.5 7.6 %gather_fusion.1 = bf16[128,64,576]{2,1,0:T(8,128)(2,1)} fusion(bf16[32,64,576]{2,1,0:T(8,128)(2,1)S(1)} %bitcast.67, s32[1024]{0:T(1024)S(1)} %pad_clamp_fusion), kind=kCustom, calls=%fused_computation.1 | custom fusion | bytes 18874880 | tf_op jit(solution)/shard_map/gather | solution.py:82
  62.1 2.7 all-to-all-done
  64.8 5.1 %all-to-all-start.2 = ((bf16[16,8,64,576]{3,2,1,0:T(8,128)(2,1)}), bf16[16,8,64,576]{3,2,1,0:T(8,128)(2,1)}, u32[]{:S(2)}, u32[]{:S(2)}) async-start(bf16[16,8,64,576]{3,2,1,0:T(8,128)(2,1)} %bitcast.68), calls=%async_computation.2 | async-start | bytes 20971520 | tf_op jit(solution)/shard_map/all_to_all | solution.py:83
  72.0 184.8 %all-to-all-done.2 = bf16[16,8,64,576]{3,2,1,0:T(8,128)(2,1)} async-done(((bf16[16,8,64,576]{3,2,1,0:T(8,128)(2,1)}), bf16[16,8,64,576]{3,2,1,0:T(8,128)(2,1)}, u32[]{:S(2)}, u32[]{:S(2)}) %all-to-all-start.2) | async-done | bytes 9437216 | tf_op jit(solution)/shard_map/all_to_all | solution.py:83
  256.8 63.6 %while.10 = (s32[]{:T(128)}, bf16[4,128,512]{2,1,0:T(8,128)(2,1)}, pred[4,2048]{1,0:T(4,128)(4,1)S(1)}, bf16[4,128,576]{2,1,0:T(8,128)(2,1)S(1)}, s32[4,2048]{1,...) while((s32[]{:T(128)}, bf16[4,128,512]{2,1,0:T(8,128)(2,1)}, pred[4,2048]{1,0:T(4,128)(4,1)S(1)}, ...), condition=%wide.region_8.9_spmd, body=%wide.region_5.8_spmd.sunk | while | flops 572595968 | bytes 12928089 | solution.py:103
  256.8 13.3 %gather_fusion = bf16[2048,576]{1,0:T(8,128)(2,1)S(1)} fusion(bf16[8192,576]{1,0:T(8,128)(2,1)} %get-tuple-element.118, s32[2048]{0:T(1024)S(1)} %broadcast_clamp_fusion.2), kind=kCustom, calls=%fused_computation.clone.1 | custom fusion | bytes 4726784 | tf_op jit(solution)/shard_map/while/body/eval_jaxpr/gather | solution.py:93
  271.5 1.2 fusion.56
  272.8 13.3 %gather_fusion = bf16[2048,576]{1,0:T(8,128)(2,1)S(1)} fusion(bf16[8192,576]{1,0:T(8,128)(2,1)} %get-tuple-element.118, s32[2048]{0:T(1024)S(1)} %broadcast_clamp_fusion.2), kind=kCustom, calls=%fused_computation.clone.1 | custom fusion | bytes 4726784 | tf_op jit(solution)/shard_map/while/body/eval_jaxpr/gather | solution.py:93
  287.5 1.2 fusion.56
  288.7 13.3 %gather_fusion = bf16[2048,576]{1,0:T(8,128)(2,1)S(1)} fusion(bf16[8192,576]{1,0:T(8,128)(2,1)} %get-tuple-element.118, s32[2048]{0:T(1024)S(1)} %broadcast_clamp_fusion.2), kind=kCustom, calls=%fused_computation.clone.1 | custom fusion | bytes 4726784 | tf_op jit(solution)/shard_map/while/body/eval_jaxpr/gather | solution.py:93
  304.6 13.3 %gather_fusion = bf16[2048,576]{1,0:T(8,128)(2,1)S(1)} fusion(bf16[8192,576]{1,0:T(8,128)(2,1)} %get-tuple-element.118, s32[2048]{0:T(1024)S(1)} %broadcast_clamp_fusion.2), kind=kCustom, calls=%fused_computation.clone.1 | custom fusion | bytes 4726784 | tf_op jit(solution)/shard_map/while/body/eval_jaxpr/gather | solution.py:93
  320.4 2.3 copy.54
  322.8 45.6 %all-to-all-start.3 = ((bf16[4,128,512]{2,0,1:T(4,128)(2,1)}), bf16[4,128,512]{2,0,1:T(4,128)(2,1)S(1)}, u32[]{:S(2)}, u32[]{:S(2)}) async-start(bf16[4,128,512]{2,0,1:T(4,128)(2,1)} %copy.54), calls=%async_computation.3 | async-start | bytes 1048576 | tf_op jit(solution)/shard_map/all_to_all | solution.py:104
  369.7 13.0 %all-to-all-done.3 = bf16[4,128,512]{2,0,1:T(4,128)(2,1)S(1)} async-done(((bf16[4,128,512]{2,0,1:T(4,128)(2,1)}), bf16[4,128,512]{2,0,1:T(4,128)(2,1)S(1)}, u32[]{:S(2)}, u32[]{:S(2)}) %all-to-all-start.3) | async-done | bytes 524320 | tf_op jit(solution)/shard_map/all_to_all | solution.py:104
  383.3 8.0 %fusion.23 = f32[64,7168]{1,0:T(8,128)S(1)} fusion(bf16[1024,7168]{1,0:T(8,128)(2,1)} %param.17, bf16[8,8,8,128]{3,2,1,0:T(8,128)(2,1)S(1)} %fusion.20), kind=kOutput, calls=%fused_computation.37 | convolution fusion | flops 939524096 | bytes 16646144 | tf_op jit(solution)/shard_map/dot_general | solution.py:110
  391.3 73.7 %all-reduce.2 = bf16[64,7168]{1,0:T(8,128)(2,1)} all-reduce(f32[64,7168]{1,0:T(8,128)S(1)} %fusion.23), channel_id=2, replica_groups=mesh['groups'=2,'ctx'=16] {'ctx'}, use_global_device_ids=true, to_apply=%region_9.10.clone | all-reduce | flops 458752 | bytes 2752512
  465.1 1.6 dynamic-slice_convert_fusion
  (91 shorter events, 20.0 us)
Async XLA Ops:
  0.0 38.0 %copy-start = (bf16[8,128,512]{2,1,0:T(8,128)(2,1)S(1)}, bf16[8,128,512]{2,1,0:T(8,128)(2,1)}, u32[]{:S(2)}) copy-start(bf16[8,128,512]{2,1,0:T(8,128)(2,1)} %param.15) | copy-start | bytes 3145732
  2.9 41.1 %all-to-all-start.1 = ((s32[16,1,8]{2,1,0:T(1,128)}), s32[16,1,8]{2,1,0:T(1,128)S(1)}, u32[]{:S(2)}, u32[]{:S(2)}) async-start(s32[16,1,8]{2,1,0:T(1,128)} %bitcast.18), calls=%async_computation.1 | async-start | bytes 16384 | tf_op jit(solution)/shard_map/all_to_all | solution.py:82
  38.6 1.2 copy-start.5
  38.6 1.8 slice-start
  39.8 3.1 slice-start.1
  44.0 20.9 %all-to-all-start = ((bf16[64,8,576]{2,1,0:T(8,128)(2,1)}), bf16[64,8,576]{2,1,0:T(8,128)(2,1)}, u32[]{:S(2)}, u32[]{:S(2)}) async-start(bf16[64,8,576]{2,1,0:T(8,128)(2,1)} %copy.45), calls=%async_computation | async-start | bytes 1310720 | tf_op jit(solution)/shard_map/all_to_all | solution.py:81
  48.2 4.7 %copy-start.2 = (bf16[2048,512]{1,0:T(8,128)(2,1)S(1)}, bf16[2048,512]{1,0:T(8,128)(2,1)}, u32[]{:S(2)}) copy-start(bf16[2048,512]{1,0:T(8,128)(2,1)} %copy.59) | copy-start | bytes 6291460
  52.9 1.0 copy-start.3
  64.8 5.2 %copy-start.6 = (s32[4,32]{1,0:T(4,128)S(1)}, s32[4,32]{1,0:T(4,128)}, u32[]{:S(2)}) copy-start(s32[4,32]{1,0:T(4,128)} %param.20) | copy-start | bytes 1540
  64.8 5.5 %copy-start.7 = (s32[4]{0:T(128)S(1)}, s32[4]{0:T(128)}, u32[]{:S(2)}) copy-start(s32[4]{0:T(128)} %param.21) | copy-start | bytes 52
  64.8 192.0 %all-to-all-start.2 = ((bf16[16,8,64,576]{3,2,1,0:T(8,128)(2,1)}), bf16[16,8,64,576]{3,2,1,0:T(8,128)(2,1)}, u32[]{:S(2)}, u32[]{:S(2)}) async-start(bf16[16,8,64,576]{3,2,1,0:T(8,128)(2,1)} %bitcast.68), calls=%async_computation.2 | async-start | bytes 20971520 | tf_op jit(solution)/shard_map/all_to_all | solution.py:83
  256.8 111.6 %copy-start.8 = (u32[32]{0:T(128)S(1)}, u32[32]{0:T(128)}, u32[]{:S(2)}) copy-start(u32[32]{0:T(128)} %constant.72) | copy-start | bytes 388
  320.4 62.6 %copy-start.4 = (bf16[8,512,128]{2,1,0:T(8,128)(2,1)S(1)}, bf16[8,512,128]{2,1,0:T(8,128)(2,1)}, u32[]{:S(2)}) copy-start(bf16[8,512,128]{2,1,0:T(8,128)(2,1)} %param.16) | copy-start | bytes 3145732
  322.8 59.9 %all-to-all-start.3 = ((bf16[4,128,512]{2,0,1:T(4,128)(2,1)}), bf16[4,128,512]{2,0,1:T(4,128)(2,1)S(1)}, u32[]{:S(2)}, u32[]{:S(2)}) async-start(bf16[4,128,512]{2,0,1:T(4,128)(2,1)} %copy.54), calls=%async_computation.3 | async-start | bytes 1048576 | tf_op jit(solution)/shard_map/all_to_all | solution.py:104
  383.3 83.3 %copy-start.1 = (bf16[8,128,512]{2,1,0:T(8,128)(2,1)S(1)}, bf16[8,128,512]{2,1,0:T(8,128)(2,1)}, u32[]{:S(2)}) copy-start(bf16[8,128,512]{2,1,0:T(8,128)(2,1)} %param.15) | copy-start | bytes 3145732
where the time goes:
time: 468 us; the launch traced here: 467 us
  waiting for transfers between devices  201 us (43%)
  blocking collectives  95.9 us (20%)
  local copies, waits for them, and re-layouts  78.1 us (17%)
  starting transfers between devices  62.5 us (13%)
  matrix products  20.8 us (4%)
  other arithmetic  7.66 us (2%)
    all_to_all x1, waiting for transfers between devices, local(): lax.all_to_all(served, 'ctx', split_axis=0, concat_axis=0, tiled=True)  185 us
    unnamed x1, blocking collectives  73.7 us
    gather x4, local copies, waits for them, and re-layouts, attend(): key_rows = fetched_rows[token_rows]  53.1 us
    all_to_all x1, starting transfers between devices, local(): lax.all_to_all(latent_out, 'ctx', split_axis=1, concat_axis=0, tiled=True)  45.6 us
    all_gather x1, blocking collectives, local(): shard_piece = lax.all_gather(normed, 'ctx', axis=0, tiled=True)  22.2 us
    all_to_all x1, waiting for transfers between devices, local(): lax.all_to_all(latent_out, 'ctx', split_axis=1, concat_axis=0, tiled=True)  13 us
  transfers between devices with their start and end apart: 4, of which 3 were waited for; matrix products, arithmetic and copies ran while one was open for 6% of the time, Pallas kernels for 0%

commit v1 on v0

--- a/solution.py
+++ b/solution.py
@@ -101,7 +101,10 @@
         ).astype(jnp.bfloat16)
 
     latent_out = lax.map(attend, (queries, token_index, live_tokens))
-    head_out = lax.all_to_all(latent_out, "ctx", split_axis=1, concat_axis=0, tiled=True)
+    head_out = jnp.concatenate(
+        lax.all_to_all(jnp.stack(jnp.split(latent_out, lax.axis_size("ctx"), axis=1)), "ctx", 0, 0),
+        axis=0,
+    )
     head_values = jnp.einsum(
         "qhc,hcv->qhv", head_out, w_uv, preferred_element_type=jnp.float32
     ).astype(jnp.bfloat16)

time: 468 us -> 489 us (1.045)
  local copies, waits for them, and re-layouts: 78.1 us -> 97.3 us
    unnamed x23 -> x36, local copies, waits for them, and re-layouts: 4.63 us -> 25 us
where the time goes in v1:
time: 489 us; the launch traced here: 487 us
  waiting for transfers between devices  201 us (41%)
  local copies, waits for them, and re-layouts  97.3 us (20%)
  blocking collectives  95.9 us (20%)
  starting transfers between devices  62.5 us (13%)
  matrix products  22.1 us (5%)
  other arithmetic  7.66 us (2%)
    all_to_all x1, waiting for transfers between devices, local(): lax.all_to_all(served, 'ctx', split_axis=0, concat_axis=0, tiled=True)  185 us
    unnamed x1, blocking collectives  73.7 us
    gather x4, local copies, waits for them, and re-layouts, attend(): key_rows = fetched_rows[token_rows]  53.1 us
    all_to_all x1, starting transfers between devices, local(): lax.all_to_all(jnp.stack(jnp.split(latent_out, lax.axis_size('ctx'), axis...  45.6 us
    unnamed x36, local copies, waits for them, and re-layouts  25 us
    all_gather x1, blocking collectives, local(): shard_piece = lax.all_gather(normed, 'ctx', axis=0, tiled=True)  22.2 us
    all_to_all x1, waiting for transfers between devices, local(): lax.all_to_all(jnp.stack(jnp.split(latent_out, lax.axis_size('ctx'), axis...  13 us
  transfers between devices with their start and end apart: 4, of which 3 were waited for; matrix products, arithmetic and copies ran while one was open for 6% of the time, Pallas kernels for 0%

profile of v1, /device:TPU:0, one launch (start us, length us, event | category | flops | bytes accessed | tf_op | source)
XLA Modules:
  0.0 487.0 jit_solution(8213288325836384564)
XLA Ops:
  2.9 7.4 %all-to-all-start.1 = ((s32[16,1,8]{2,1,0:T(1,128)}), s32[16,1,8]{2,1,0:T(1,128)S(1)}, u32[]{:S(2)}, u32[]{:S(2)}) async-start(s32[16,1,8]{2,1,0:T(1,128)} %bitcast.33), calls=%async_computation.1 | async-start | bytes 16384 | tf_op jit(solution)/shard_map/all_to_all | solution.py:82
  12.0 22.2 %all-gather = bf16[16,4,1536]{2,1,0:T(4,128)(2,1)S(1)} all-gather(bf16[1,4,1536]{2,1,0:T(4,128)(2,1)S(1)} %fusion.31), channel_id=1, replica_groups=mesh['groups'=2,'ctx'=16] {'ctx'}, dimensions={0}, use_global_device_ids=true | all-gather | bytes 208896 | tf_op jit(solution)/shard_map/all_gather | solution.py:69
  34.2 3.3 fusion.40
  40.4 2.5 copy.58
  44.0 4.3 all-to-all-start
  48.2 4.7 broadcast_in_dim.79
  54.5 7.6 %gather_fusion.1 = bf16[128,64,576]{2,1,0:T(8,128)(2,1)} fusion(bf16[32,64,576]{2,1,0:T(8,128)(2,1)S(1)} %bitcast.93, s32[1024]{0:T(1024)S(1)} %pad_clamp_fusion), kind=kCustom, calls=%fused_computation.1 | custom fusion | bytes 18874880 | tf_op jit(solution)/shard_map/gather | solution.py:82
  62.1 2.7 all-to-all-done
  64.8 5.1 %all-to-all-start.2 = ((bf16[16,8,64,576]{3,2,1,0:T(8,128)(2,1)}), bf16[16,8,64,576]{3,2,1,0:T(8,128)(2,1)}, u32[]{:S(2)}, u32[]{:S(2)}) async-start(bf16[16,8,64,576]{3,2,1,0:T(8,128)(2,1)} %bitcast.94), calls=%async_computation.2 | async-start | bytes 20971520 | tf_op jit(solution)/shard_map/all_to_all | solution.py:83
  72.0 184.8 %all-to-all-done.2 = bf16[16,8,64,576]{3,2,1,0:T(8,128)(2,1)} async-done(((bf16[16,8,64,576]{3,2,1,0:T(8,128)(2,1)}), bf16[16,8,64,576]{3,2,1,0:T(8,128)(2,1)}, u32[]{:S(2)}, u32[]{:S(2)}) %all-to-all-start.2) | async-done | bytes 9437216 | tf_op jit(solution)/shard_map/all_to_all | solution.py:83
  256.8 63.6 %while.10 = (s32[]{:T(128)}, bf16[4,128,512]{2,1,0:T(8,128)(2,1)}, pred[4,2048]{1,0:T(4,128)(4,1)S(1)}, bf16[4,128,576]{2,1,0:T(8,128)(2,1)S(1)}, s32[4,2048]{1,...) while((s32[]{:T(128)}, bf16[4,128,512]{2,1,0:T(8,128)(2,1)}, pred[4,2048]{1,0:T(4,128)(4,1)S(1)}, ...), condition=%wide.region_8.9_spmd, body=%wide.region_5.8_spmd.sunk | while | flops 572595968 | bytes 12928089 | solution.py:103
  256.8 13.3 %gather_fusion = bf16[2048,576]{1,0:T(8,128)(2,1)S(1)} fusion(bf16[8192,576]{1,0:T(8,128)(2,1)} %get-tuple-element.118, s32[2048]{0:T(1024)S(1)} %broadcast_clamp_fusion.2), kind=kCustom, calls=%fused_computation.clone.1 | custom fusion | bytes 4726784 | tf_op jit(solution)/shard_map/while/body/eval_jaxpr/gather | solution.py:93
  272.8 13.3 %gather_fusion = bf16[2048,576]{1,0:T(8,128)(2,1)S(1)} fusion(bf16[8192,576]{1,0:T(8,128)(2,1)} %get-tuple-element.118, s32[2048]{0:T(1024)S(1)} %broadcast_clamp_fusion.2), kind=kCustom, calls=%fused_computation.clone.1 | custom fusion | bytes 4726784 | tf_op jit(solution)/shard_map/while/body/eval_jaxpr/gather | solution.py:93
  288.7 13.3 %gather_fusion = bf16[2048,576]{1,0:T(8,128)(2,1)S(1)} fusion(bf16[8192,576]{1,0:T(8,128)(2,1)} %get-tuple-element.118, s32[2048]{0:T(1024)S(1)} %broadcast_clamp_fusion.2), kind=kCustom, calls=%fused_computation.clone.1 | custom fusion | bytes 4726784 | tf_op jit(solution)/shard_map/while/body/eval_jaxpr/gather | solution.py:93
  304.6 13.3 %gather_fusion = bf16[2048,576]{1,0:T(8,128)(2,1)S(1)} fusion(bf16[8192,576]{1,0:T(8,128)(2,1)} %get-tuple-element.118, s32[2048]{0:T(1024)S(1)} %broadcast_clamp_fusion.2), kind=kCustom, calls=%fused_computation.clone.1 | custom fusion | bytes 4726784 | tf_op jit(solution)/shard_map/while/body/eval_jaxpr/gather | solution.py:93
  327.2 1.4 constant_dynamic-update-slice_fusion.10
  330.0 1.4 constant_dynamic-update-slice_fusion.8
  334.1 1.4 constant_dynamic-update-slice_fusion.5
  342.2 45.6 %all-to-all-start.3 = ((bf16[16,4,8,512]{3,2,1,0:T(8,128)(2,1)}), bf16[16,4,8,512]{3,2,1,0:T(8,128)(2,1)S(1)}, u32[]{:S(2)}, u32[]{:S(2)}) async-start(bf16[16,4,8,512]{3,2,1,0:T(8,128)(2,1)} %constant_dynamic-update-slice_fusion), calls=%async_computation.3 | async-start | bytes 1048576 | tf_op jit(solution)/shard_map/all_to_all | solution.py:105
  389.1 13.0 %all-to-all-done.3 = bf16[16,4,8,512]{3,2,1,0:T(8,128)(2,1)S(1)} async-done(((bf16[16,4,8,512]{3,2,1,0:T(8,128)(2,1)}), bf16[16,4,8,512]{3,2,1,0:T(8,128)(2,1)S(1)}, u32[]{:S(2)}, u32[]{:S(2)}) %all-to-all-start.3) | async-done | bytes 524320 | tf_op jit(solution)/shard_map/all_to_all | solution.py:105
  402.1 1.6 fusion.20
  403.8 8.0 %fusion.24 = f32[64,7168]{1,0:T(8,128)S(1)} fusion(bf16[1024,7168]{1,0:T(8,128)(2,1)} %param.17, bf16[8,8,8,128]{3,2,1,0:T(8,128)(2,1)S(1)} %fusion.20), kind=kOutput, calls=%fused_computation.37 | convolution fusion | flops 939524096 | bytes 16646144 | tf_op jit(solution)/shard_map/dot_general | solution.py:113
  411.8 73.7 %all-reduce.2 = bf16[64,7168]{1,0:T(8,128)(2,1)} all-reduce(f32[64,7168]{1,0:T(8,128)S(1)} %fusion.24), channel_id=2, replica_groups=mesh['groups'=2,'ctx'=16] {'ctx'}, use_global_device_ids=true, to_apply=%region_9.10.clone | all-reduce | flops 458752 | bytes 2752512
  485.5 1.6 dynamic-slice_convert_fusion
  (102 shorter events, 40.6 us)
Async XLA Ops:
  0.0 38.0 %copy-start = (bf16[8,128,512]{2,1,0:T(8,128)(2,1)S(1)}, bf16[8,128,512]{2,1,0:T(8,128)(2,1)}, u32[]{:S(2)}) copy-start(bf16[8,128,512]{2,1,0:T(8,128)(2,1)} %param.15) | copy-start | bytes 3145732
  2.9 41.1 %all-to-all-start.1 = ((s32[16,1,8]{2,1,0:T(1,128)}), s32[16,1,8]{2,1,0:T(1,128)S(1)}, u32[]{:S(2)}, u32[]{:S(2)}) async-start(s32[16,1,8]{2,1,0:T(1,128)} %bitcast.33), calls=%async_computation.1 | async-start | bytes 16384 | tf_op jit(solution)/shard_map/all_to_all | solution.py:82
  38.6 1.2 copy-start.4
  38.6 1.8 slice-start
  39.8 3.1 slice-start.1
  44.0 20.9 %all-to-all-start = ((bf16[64,8,576]{2,1,0:T(8,128)(2,1)}), bf16[64,8,576]{2,1,0:T(8,128)(2,1)}, u32[]{:S(2)}, u32[]{:S(2)}) async-start(bf16[64,8,576]{2,1,0:T(8,128)(2,1)} %copy.44), calls=%async_computation | async-start | bytes 1310720 | tf_op jit(solution)/shard_map/all_to_all | solution.py:81
  48.2 4.7 copy-start.2
  52.9 1.0 copy-start.3
  64.8 5.2 %copy-start.5 = (s32[4,32]{1,0:T(4,128)S(1)}, s32[4,32]{1,0:T(4,128)}, u32[]{:S(2)}) copy-start(s32[4,32]{1,0:T(4,128)} %param.20) | copy-start | bytes 1540
  64.8 5.5 %copy-start.6 = (s32[4]{0:T(128)S(1)}, s32[4]{0:T(128)}, u32[]{:S(2)}) copy-start(s32[4]{0:T(128)} %param.21) | copy-start | bytes 52
  64.8 192.0 %all-to-all-start.2 = ((bf16[16,8,64,576]{3,2,1,0:T(8,128)(2,1)}), bf16[16,8,64,576]{3,2,1,0:T(8,128)(2,1)}, u32[]{:S(2)}, u32[]{:S(2)}) async-start(bf16[16,8,64,576]{3,2,1,0:T(8,128)(2,1)} %bitcast.94), calls=%async_computation.2 | async-start | bytes 20971520 | tf_op jit(solution)/shard_map/all_to_all | solution.py:83
  256.8 131.1 %copy-start.7 = (u32[32]{0:T(128)S(1)}, u32[32]{0:T(128)}, u32[]{:S(2)}) copy-start(u32[32]{0:T(128)} %constant.72) | copy-start | bytes 388
  342.2 59.9 %all-to-all-start.3 = ((bf16[16,4,8,512]{3,2,1,0:T(8,128)(2,1)}), bf16[16,4,8,512]{3,2,1,0:T(8,128)(2,1)S(1)}, u32[]{:S(2)}, u32[]{:S(2)}) async-start(bf16[16,4,8,512]{3,2,1,0:T(8,128)(2,1)} %constant_dynamic-update-slice_fusion), calls=%async_computation.3 | async-start | bytes 1048576 | tf_op jit(solution)/shard_map/all_to_all | solution.py:105
  403.7 83.3 %copy-start.1 = (bf16[8,128,512]{2,1,0:T(8,128)(2,1)S(1)}, bf16[8,128,512]{2,1,0:T(8,128)(2,1)}, u32[]{:S(2)}) copy-start(bf16[8,128,512]{2,1,0:T(8,128)(2,1)} %param.15) | copy-start | bytes 3145732
